TPU v7x, 32 devices: a whole 2x2x4 slice. The times are simulated.
32 devices in a mesh: mom: 2 (over x), pts: 16 (over z, y, core).
Axes of the slice: x: 2, y: 2, z: 4, core: 2. Of those that a mesh axis runs over, the one named last changes fastest.
Arguments:
- amplitudes: bfloat16 [2, 2, 1, 256, 64, 128], P(None, None, None, 'mom'), may hold values from -6 to 6
- val_orbitals: bfloat16 [2, 256, 64, 512], P(None, 'mom'), may hold values from -0.25 to 0.25
- cond_orbitals: bfloat16 [2, 256, 512, 128], P(None, 'mom', 'pts'), may hold values from -0.25 to 0.25
- screened: bfloat16 [2, 256, 512, 512], P(None, None, ('pts', 'mom')), may hold values from -12 to 12
- val_energy: float32 [256, 64], P('mom', 'pts'), may hold values from -2 to -0.5
- cond_energy: float32 [256, 128], P('mom'), may hold values from 0.5 to 2
- grid_of_slot: int32 [256], replicated, may hold values from 0 to 255, as said below
- opposite_slot: int32 [256], P('mom'), may hold values from 0 to 255, as said below
Outputs:
- applied: float32 [2, 2, 1, 256, 64, 128], P(None, None, None, 'mom', 'pts')
Inputs may be any that keep to these rules, and one draw needn't show every extreme that they name: `grid_of_slot`: a permutation of the grid indices. opposite_slot[s] is the slot whose grid index is 255 - grid_of_slot[s]; it is never s, and s and opposite_slot[s] lie in aligned blocks of 128 slots whose first slots differ by 128.
All inputs are finite; a program needn't handle non-finite values.
Results may differ from a plain program's by a relative error of at most 0.006.
Values may be sent and summed in bfloat16 or wider, within the bound.
No kernel may reach another device: no remote copies, remote signals or barrier semaphores. Data moves between devices by JAX's collectives and lax.ppermute only.
A program may use at most 256 MiB of HBM per device.

v0:
```python
import math
import jax
import jax.numpy as jnp
from jax import lax
from jax.sharding import PartitionSpec as P


def partner_2(value, axis, apart):
    mask = 2**apart
    pairs = [(source, source ^ mask) for source in range(lax.axis_size(axis))]
    return lax.ppermute(value, axis, pairs)


def complex_mix(formula, left, right, left_sign, right_sign):
    real_real = jnp.einsum(formula, left[0], right[0], preferred_element_type=jnp.float32)
    imag_imag = jnp.einsum(formula, left[1], right[1], preferred_element_type=jnp.float32)
    real_imag = jnp.einsum(formula, left[0], right[1], preferred_element_type=jnp.float32)
    imag_real = jnp.einsum(formula, left[1], right[0], preferred_element_type=jnp.float32)
    return jnp.stack(
        [
            real_real - left_sign * right_sign * imag_imag,
            right_sign * real_imag + left_sign * imag_real,
        ]
    )


def on_device(
    amplitudes,
    val_orbitals,
    cond_orbitals,
    screened,
    val_energy,
    cond_energy,
    grid_of_slot,
    opposite_slot,
):
    slots_here = opposite_slot.shape[0]
    total_slots = grid_of_slot.shape[0]
    rows_here = val_energy.shape[1]
    frequency = jnp.arange(total_slots, dtype=jnp.int32)
    phases = frequency[:, None] * grid_of_slot[None, :] % total_slots
    angles = phases.astype(jnp.float32) * (2.0 * math.pi / total_slots)
    cosine_table = jnp.cos(angles).astype(jnp.bfloat16)
    sine_table = jnp.sin(angles).astype(jnp.bfloat16)
    half_product = complex_mix("bnkvc,kuc->bnkvu", amplitudes, cond_orbitals, 1.0, 1.0).astype(
        jnp.bfloat16
    )
    pair_values = complex_mix("bnkvu,kvm->bnkum", half_product, val_orbitals, 1.0, -1.0).astype(
        jnp.bfloat16
    )
    flattened = pair_values.reshape(pair_values.shape[:4] + (-1,))
    weights = screened.reshape(2, total_slots, -1)
    inverse_count = 1.0 / total_slots
    whole_k = lax.all_to_all(flattened, "mom", split_axis=4, concat_axis=3, tiled=True)
    spec_real = jnp.einsum(
        "fs,bnsc->bnfc", cosine_table, whole_k[0], preferred_element_type=jnp.float32
    ) + jnp.einsum("fs,bnsc->bnfc", sine_table, whole_k[1], preferred_element_type=jnp.float32)
    spec_imag = jnp.einsum(
        "fs,bnsc->bnfc", cosine_table, whole_k[1], preferred_element_type=jnp.float32
    ) - jnp.einsum("fs,bnsc->bnfc", sine_table, whole_k[0], preferred_element_type=jnp.float32)
    prod_real = (weights[0] * spec_real - weights[1] * spec_imag).astype(jnp.bfloat16)
    prod_imag = (weights[0] * spec_imag + weights[1] * spec_real).astype(jnp.bfloat16)
    back_real = (
        jnp.einsum("fs,bnfc->bnsc", cosine_table, prod_real, preferred_element_type=jnp.float32)
        - jnp.einsum("fs,bnfc->bnsc", sine_table, prod_imag, preferred_element_type=jnp.float32)
    ) * inverse_count
    back_imag = (
        jnp.einsum("fs,bnfc->bnsc", cosine_table, prod_imag, preferred_element_type=jnp.float32)
        + jnp.einsum("fs,bnfc->bnsc", sine_table, prod_real, preferred_element_type=jnp.float32)
    ) * inverse_count
    field_pts = lax.all_to_all(
        jnp.stack([back_real, back_imag]).astype(jnp.bfloat16),
        "mom",
        split_axis=3,
        concat_axis=4,
        tiled=True,
    )
    field_pts = field_pts.reshape(pair_values.shape)
    weighted = complex_mix("bnkum,kvm->bnkvu", field_pts, val_orbitals, 1.0, 1.0).astype(
        jnp.bfloat16
    )
    rows_mine = lax.all_to_all(weighted, "pts", split_axis=4, concat_axis=5, tiled=True)
    band_values = complex_mix(
        "bnkvu,kuc->bnkvc",
        rows_mine,
        lax.all_gather(cond_orbitals, "pts", axis=2, tiled=True),
        1.0,
        -1.0,
    )
    top_bit = lax.axis_size("mom").bit_length() - 2
    partner = partner_2(band_values.astype(jnp.bfloat16), "mom", top_bit).astype(band_values.dtype)
    mirrored = jnp.take(partner, opposite_slot % slots_here, axis=3)
    start_row = lax.axis_index("pts") * rows_here
    own_rows = lax.dynamic_slice_in_dim(amplitudes, start_row, rows_here, 4).astype(jnp.float32)
    energy_gap = cond_energy[:, None, :] - val_energy[:, :, None]
    result_real = energy_gap * own_rows[0, 0] - band_values[0, 0] - mirrored[0, 1]
    result_imag = energy_gap * own_rows[1, 0] - band_values[1, 0] + mirrored[1, 1]
    anti_real = -energy_gap * own_rows[0, 1] + band_values[0, 1] + mirrored[0, 0]
    anti_imag = -energy_gap * own_rows[1, 1] + band_values[1, 1] - mirrored[1, 0]
    return jnp.stack([jnp.stack([result_real, anti_real]), jnp.stack([result_imag, anti_imag])])


def solution(mesh):
    in_specs = (
        P(None, None, None, "mom", None, None),
        P(None, "mom", None, None),
        P(None, "mom", "pts", None),
        P(None, None, ("pts", "mom"), None),
        P("mom", "pts"),
        P("mom", None),
        P(),
        P("mom"),
    )
    out_specs = P(None, None, None, "mom", "pts", None)
    return jax.shard_map(
        on_device, mesh=mesh, in_specs=in_specs, out_specs=out_specs, check_vma=False
    )
```

profile of v0, /device:TPU:0, one launch (start us, length us, event | category | flops | bytes accessed | tf_op | source)
XLA Modules:
  0.0 1007.6 jit_solution(14866260467784046337)
XLA Ops:
  40.7 14.0 %fusion.34 = bf16[2,1,128,32,512]{4,3,0,2,1:T(8,128)(2,1)} fusion(f32[128,2,32,512]{3,2,1,0:T(8,128)} %fusion.17, bf16[2,128,64,32]{2,3,0,1:T(8,128)(2,1)} %fusion.45, bf16[2,128,64,512]{3,2,1,0:T(8,128)(2,1)} %param.9), kind=kOutput, calls=%fused_computation.51 | convolution fusion | flops 549453824 | bytes 35651584 | tf_op jit(solution)/shard_map/bnkvu,kvm->bnkum/dot_general | solution.py:16
  54.7 16.5 %copy.203 = bf16[2,1,128,32,512]{2,0,4,3,1:T(2,128)(2,1)} copy(bf16[2,1,128,32,512]{4,3,0,2,1:T(8,128)(2,1)} %fusion.34) | data formatting | bytes 16777216 | tf_op jit(solution)/shard_map/stack | solution.py:19
  71.2 12.1 %fusion.23 = f32[128,2,32,512]{3,2,1,0:T(8,128)} fusion(bf16[2,128,64,32]{2,3,0,1:T(8,128)(2,1)S(1)} %copy-done.4, bf16[2,128,64,512]{3,2,1,0:T(8,128)(2,1)} %param.9), kind=kOutput, calls=%fused_computation.40 | convolution fusion | flops 536870912 | bytes 26214400 | tf_op jit(solution)/shard_map/bnkvu,kvm->bnkum/dot_general | solution.py:17
  83.4 12.9 %fusion.37 = bf16[2,1,128,32,512]{4,3,0,2,1:T(8,128)(2,1)} fusion(bf16[2,128,64,32]{2,3,0,1:T(8,128)(2,1)S(1)} %copy-done.2, bf16[2,128,64,512]{3,2,1,0:T(8,128)(2,1)} %param.9, f32[128,2,32,512]{3,2,1,0:T(8,128)} %fusion.23), kind=kOutput, calls=%fused_computation.52 | convolution fusion | flops 549453824 | bytes 34603008 | tf_op jit(solution)/shard_map/bnkvu,kvm->bnkum/dot_general | solution.py:18
  96.3 15.7 %copy.204 = bf16[2,1,128,32,512]{2,0,4,3,1:T(2,128)(2,1)} copy(bf16[2,1,128,32,512]{4,3,0,2,1:T(8,128)(2,1)} %fusion.37) | data formatting | bytes 16777216 | tf_op jit(solution)/shard_map/stack | solution.py:19
  112.0 26.4 %pad_maximum_fusion = bf16[2,2,1,128,16384]{3,1,2,0,4:T(2,128)(2,1)} fusion(bf16[1,2,1,128,16384]{3,1,2,0,4:T(2,128)(2,1)} %bitcast.316, bf16[1,2,1,128,16384]{3,1,2,0,4:T(2,128)(2,1)} %bitcast.315), kind=kLoop, calls=%fused_computation.3 | loop fusion | flops 8388608 | bytes 33554432 | tf_op jit(solution)/shard_map/stack | solution.py:19
  148.2 12.1 %slice_convert_fusion.1 = (f32[1,256,16,512]{3,2,1,0:T(8,128)}, f32[1,256,16,512]{3,2,1,0:T(8,128)}) fusion(bf16[2,256,16,512]{3,2,1,0:T(8,128)(2,1)} %param.11), kind=kLoop, calls=%fused_computation.61 | loop fusion | flops 4194304 | bytes 25165824 | tf_op jit(solution)/shard_map/convert_element_type | solution.py:61
  160.3 9.9 copy.202
  170.2 10.0 copy.205
  180.2 150.9 %all-to-all-done = bf16[2,2,1,128,16384]{3,1,2,0,4:T(2,128)(2,1)} async-done(((bf16[2,2,1,128,16384]{3,1,2,0,4:T(2,128)(2,1)}), bf16[2,2,1,128,16384]{3,1,2,0,4:T(2,128)(2,1)}, u32[]{:S(2)}, u32[]{:S(2)}) %all-to-all-start) | async-done | bytes 16777248 | tf_op jit(solution)/shard_map/all_to_all | solution.py:54
  331.1 28.1 %copy.246 = bf16[2,2,1,128,2,8192]{3,4,5,1,2,0:T(2,128)(2,1)S(1)} copy(bf16[2,2,1,128,2,8192]{3,1,0,5,4,2:T(2,128)(2,1)} %bitcast.38) | data formatting | bytes 33554432 | tf_op jit(solution)/shard_map/all_to_all | solution.py:54
  359.2 13.0 %fusion.133 = (bf16[1,2,1,2,128,8192]{4,3,5,1,2,0:T(2,128)(2,1)}, bf16[1,2,1,2,128,8192]{4,3,5,1,2,0:T(2,128)(2,1)}) fusion(bf16[2,2,1,2,128,8192]{4,3,5,1,2,0:T(2,128)(2,1)S(1)} %bitcast.312), kind=kLoop, calls=%fused_computation.179 | loop fusion | bytes 33554432 | tf_op jit(solution)/shard_map/slice | solution.py:57
  372.2 14.1 %reshape.539 = bf16[2,256,8192]{1,2,0:T(8,128)(2,1)} reshape(bf16[1,2,1,2,128,8192]{4,3,5,1,2,0:T(2,128)(2,1)} %get-tuple-element.15) | data formatting | bytes 16777216 | tf_op jit(solution)/shard_map/reshape.28
  386.3 14.2 %reshape.538 = bf16[2,256,8192]{1,2,0:T(8,128)(2,1)} reshape(bf16[1,2,1,2,128,8192]{4,3,5,1,2,0:T(2,128)(2,1)} %get-tuple-element.16) | data formatting | bytes 16777216 | tf_op jit(solution)/shard_map/reshape.24
  400.5 12.5 %fusion.91 = f32[2,8192,256]{2,1,0:T(8,128)} fusion(bf16[2,256,8192]{1,2,0:T(8,128)(2,1)} %reshape.539, s32[256]{0:T(256)S(1)} %copy-done.6), kind=kOutput, calls=%fused_computation.134 | convolution fusion | flops 2148466688 | bytes 25166848 | tf_op jit(solution)/shard_map/fs,bnsc->bnfc/dot_general | solution.py:58
  422.1 14.8 %convolution_subtract_fusion = f32[2,8192,256]{2,1,0:T(8,128)} fusion(f32[2,8192,256]{2,1,0:T(8,128)} %fusion.91, bf16[2,256,8192]{1,2,0:T(8,128)(2,1)S(1)} %copy-done.1, s32[256]{0:T(256)S(1)} %copy-done.6), kind=kOutput, calls=%fused_computation.23 | convolution fusion | flops 2152660992 | bytes 41944064 | tf_op jit(solution)/shard_map/fs,bnsc->bnfc/dot_general | solution.py:60
  436.9 27.2 %fusion.11 = (bf16[2,256,8192]{1,2,0:T(8,128)(2,1)}, bf16[2,256,8192]{1,2,0:T(8,128)(2,1)}) fusion(f32[2,8192,256]{2,1,0:T(8,128)} %convolution_subtract_fusion, f32[256,8192]{0,1:T(8,128)} %bitcast.311, f32[256,8192]{0,1:T(8,128)} %bitcast.310, f32[2,8192,256]{2,1,0:T(8,128)} %fusion.93, bf16[2,256,8192]{1,2,0:T(8,128)(2,1)} %reshape.539, s32[256]{0:T(256)S(1)} %copy-done.6), kind=kOutput, calls=%fused_computation.28 | convolution fusion | flops 2186215424 | bytes 75498496 | tf_op jit(solution)/shard_map/fs,bnsc->bnfc/dot_general | solution.py:57
  464.1 12.5 %fusion.89 = f32[2,8192,256]{2,1,0:T(8,128)} fusion(bf16[2,256,8192]{1,2,0:T(8,128)(2,1)} %get-tuple-element.11, s32[256]{0:T(256)S(1)} %copy-done.6), kind=kOutput, calls=%fused_computation.133 | convolution fusion | flops 2148466688 | bytes 25166848 | tf_op jit(solution)/shard_map/fs,bnfc->bnsc/dot_general | solution.py:64
  485.7 13.5 %fusion.8 = bf16[1,2,1,256,8192]{3,4,1,2,0:T(8,128)(2,1)} fusion(f32[2,8192,256]{2,1,0:T(8,128)} %fusion.89, bf16[2,256,8192]{1,2,0:T(8,128)(2,1)} %get-tuple-element.12, s32[256]{0:T(256)S(1)} %copy-done.6), kind=kOutput, calls=%fused_computation.25 | convolution fusion | flops 2161049600 | bytes 33555456 | tf_op jit(solution)/shard_map/fs,bnfc->bnsc/dot_general | solution.py:65
  499.2 11.5 %fusion.9 = bf16[1,2,1,256,8192]{3,4,1,2,0:T(8,128)(2,1)} fusion(f32[2,8192,256]{2,1,0:T(8,128)} %fusion.87, bf16[2,256,8192]{1,2,0:T(8,128)(2,1)S(1)} %bitcast.309, s32[256]{0:T(256)S(1)} %copy-done.6), kind=kOutput, calls=%fused_computation.26 | convolution fusion | flops 2161049600 | bytes 33555456 | tf_op jit(solution)/shard_map/fs,bnfc->bnsc/dot_general | solution.py:69
  510.8 13.7 %pad_maximum_fusion.1 = bf16[2,2,1,256,8192]{3,4,1,2,0:T(8,128)(2,1)} fusion(bf16[1,2,1,256,8192]{3,4,1,2,0:T(8,128)(2,1)} %fusion.9, bf16[1,2,1,256,8192]{3,4,1,2,0:T(8,128)(2,1)} %fusion.8), kind=kLoop, calls=%fused_computation.4 | loop fusion | flops 8388608 | bytes 33554432 | tf_op jit(solution)/shard_map/stack | solution.py:72
  524.5 41.2 %copy.175 = bf16[2,2,1,256,8192]{4,1,2,0,3:T(2,128)(2,1)} copy(bf16[2,2,1,256,8192]{3,4,1,2,0:T(8,128)(2,1)} %pad_maximum_fusion.1) | data formatting | bytes 33554432 | tf_op jit(solution)/shard_map/stack | solution.py:72
  565.7 200.1 %all_to_all.45 = bf16[2,2,1,256,8192]{4,1,2,0,3:T(2,128)(2,1)} all-to-all(bf16[2,2,1,256,8192]{4,1,2,0,3:T(2,128)(2,1)} %copy.175), channel_id=1, replica_groups=mesh['mom'=2,'pts'=16] {'mom'}, dimensions={3} | all-to-all | bytes 33554432 | tf_op jit(solution)/shard_map/all_to_all | solution.py:71
  765.8 30.2 %copy.245 = bf16[2,2,1,2,128,8192]{5,3,1,4,2,0:T(2,128)(2,1)S(1)} copy(bf16[2,2,1,2,128,8192]{5,1,0,4,3,2:T(2,128)(2,1)} %bitcast.314) | data formatting | bytes 33554432 | tf_op jit(solution)/shard_map/all_to_all | solution.py:71
  796.1 14.9 %fusion.132 = (bf16[1,2,1,128,2,8192]{5,4,1,3,2,0:T(2,128)(2,1)}, bf16[1,2,1,128,2,8192]{5,4,1,3,2,0:T(2,128)(2,1)}) fusion(bf16[2,2,1,128,2,8192]{5,4,1,3,2,0:T(2,128)(2,1)S(1)} %bitcast.313), kind=kLoop, calls=%fused_computation.178 | loop fusion | bytes 33554432 | tf_op jit(solution)/shard_map/slice | solution.py:15
  811.0 14.3 %reshape.542 = bf16[2,128,32,512]{3,2,0,1:T(8,128)(2,1)} reshape(bf16[1,2,1,128,2,8192]{5,4,1,3,2,0:T(2,128)(2,1)} %get-tuple-element.13) | data formatting | bytes 16777216 | tf_op jit(solution)/shard_map/reshape.50
  825.2 14.3 %reshape.543 = bf16[2,128,32,512]{3,2,0,1:T(8,128)(2,1)} reshape(bf16[1,2,1,128,2,8192]{5,4,1,3,2,0:T(2,128)(2,1)} %get-tuple-element.14) | data formatting | bytes 16777216 | tf_op jit(solution)/shard_map/reshape.54
  839.5 10.1 fusion.14
  849.6 10.1 fusion.12
  868.9 10.7 %fusion.47 = bf16[1,2,1,128,64,32]{4,5,1,3,2,0:T(8,128)(2,1)} fusion(f32[128,2,32,64]{3,2,1,0:T(8,128)} %fusion.12, bf16[2,128,32,512]{3,2,0,1:T(8,128)(2,1)} %reshape.542, bf16[2,128,64,512]{3,2,1,0:T(8,128)(2,1)} %param.9), kind=kOutput, calls=%fused_computation.69 | convolution fusion | flops 537919488 | bytes 22020096 | tf_op jit(solution)/shard_map/bnkum,kvm->bnkvu/dot_general | solution.py:17
  892.1 52.0 %all_to_all.46 = bf16[2,2,1,128,64,32]{3,5,2,1,0,4:T(8,128)(2,1)S(1)} all-to-all(bf16[2,2,1,128,64,32]{3,5,2,1,0,4:T(8,128)(2,1)S(1)} %copy.177), channel_id=1, replica_groups=mesh['mom'=2,'pts'=16] {'pts'}, dimensions={4} | all-to-all | bytes 4194304 | tf_op jit(solution)/shard_map/all_to_all | solution.py:82
  980.9 12.8 %collective-permute-done = bf16[2,2,1,128,4,128]{5,3,4,2,1,0:T(8,128)(2,1)S(1)} collective-permute-done((bf16[2,2,1,128,4,128]{5,3,4,2,1,0:T(8,128)(2,1)S(1)}, bf16[2,2,1,128,4,128]{5,3,4,2,1,0:T(8,128)(2,1)S(1)}, u32[]{:S(2)}, u32[]{:S(2)}) %collective-permute-start) | collective-permute-done | bytes 524320 | tf_op jit(solution)/shard_map/ppermute | solution.py:11
  (74 shorter events, 127.3 us)
Async XLA Ops:
  6.5 942.7 %all-gather.2.cloned.1.call-start = ((), (), s32[]{:S(2)}) async-start(), calls=%async_computation.3 | async-start | bytes 35651584 | tf_op jit(solution)/shard_map/all_gather | solution.py:86
  7.3 4.6 copy-start.3
  16.0 14.9 %slice-start = ((s8[16777216]{0:T(1024)(128)(4,1)}), s8[4194304]{0:T(1024)(128)(4,1)S(1)}, s32[]{:S(2)}) async-start(s8[16777216]{0:T(1024)(128)(4,1)} %bitcast.306), calls=%async_computation.4 | async-start | bytes 8388608
  16.0 14.9 %slice-start.1 = ((s8[16777216]{0:T(1024)(128)(4,1)}), s8[4194304]{0:T(1024)(128)(4,1)S(1)}, s32[]{:S(2)}) async-start(s8[16777216]{0:T(1024)(128)(4,1)} %bitcast.306), calls=%async_computation.5 | async-start | bytes 8388608
  20.0 10.8 %slice-start.2 = ((s8[16777216]{0:T(1024)(128)(4,1)}), s8[4194304]{0:T(1024)(128)(4,1)S(1)}, s32[]{:S(2)}) async-start(s8[16777216]{0:T(1024)(128)(4,1)} %bitcast.306), calls=%async_computation.6 | async-start | bytes 8388608
  25.5 5.4 slice-start.3
  54.7 16.5 %copy-start.4 = (bf16[2,128,64,32]{2,3,0,1:T(8,128)(2,1)S(1)}, bf16[2,128,64,32]{2,3,0,1:T(8,128)(2,1)}, u32[]{:S(2)}) copy-start(bf16[2,128,64,32]{2,3,0,1:T(8,128)(2,1)} %fusion.44) | copy-start | bytes 3145732
  71.2 12.1 %copy-start.2 = (bf16[2,128,64,32]{2,3,0,1:T(8,128)(2,1)S(1)}, bf16[2,128,64,32]{2,3,0,1:T(8,128)(2,1)}, u32[]{:S(2)}) copy-start(bf16[2,128,64,32]{2,3,0,1:T(8,128)(2,1)} %fusion.45) | copy-start | bytes 3145732
  138.4 192.7 %all-to-all-start = ((bf16[2,2,1,128,16384]{3,1,2,0,4:T(2,128)(2,1)}), bf16[2,2,1,128,16384]{3,1,2,0,4:T(2,128)(2,1)}, u32[]{:S(2)}, u32[]{:S(2)}) async-start(bf16[2,2,1,128,16384]{3,1,2,0,4:T(2,128)(2,1)} %pad_maximum_fusion), calls=%async_computation | async-start | bytes 33554432 | tf_op jit(solution)/shard_map/all_to_all | solution.py:54
  386.3 14.2 %copy-start.6 = (s32[256]{0:T(256)S(1)}, s32[256]{0:T(256)}, u32[]{:S(2)}) copy-start(s32[256]{0:T(256)} %param.14) | copy-start | bytes 3076
  400.5 12.6 %copy-start.1 = (bf16[2,256,8192]{1,2,0:T(8,128)(2,1)S(1)}, bf16[2,256,8192]{1,2,0:T(8,128)(2,1)}, u32[]{:S(2)}) copy-start(bf16[2,256,8192]{1,2,0:T(8,128)(2,1)} %reshape.538) | copy-start | bytes 25165828
  464.1 12.6 %copy-start = (bf16[2,256,8192]{1,2,0:T(8,128)(2,1)S(1)}, bf16[2,256,8192]{1,2,0:T(8,128)(2,1)}, u32[]{:S(2)}) copy-start(bf16[2,256,8192]{1,2,0:T(8,128)(2,1)} %get-tuple-element.12) | copy-start | bytes 25165828
  464.1 35.1 %slice-start.4 = ((s8[8388608]{0:T(1024)(128)(4,1)}), s8[4194304]{0:T(1024)(128)(4,1)S(1)}, s32[]{:S(2)}) async-start(s8[8388608]{0:T(1024)(128)(4,1)} %bitcast.308), calls=%async_computation.8 | async-start | bytes 8388608
  476.7 22.5 %slice-start.5 = ((s8[8388608]{0:T(1024)(128)(4,1)}), s8[4194304]{0:T(1024)(128)(4,1)S(1)}, s32[]{:S(2)}) async-start(s8[8388608]{0:T(1024)(128)(4,1)} %bitcast.308), calls=%async_computation.9 | async-start | bytes 8388608
  970.4 8.9 copy-start.8
  977.5 18.9 %copy-start.5 = (f32[128,128]{1,0:T(8,128)S(1)}, f32[128,128]{1,0:T(8,128)}, u32[]{:S(2)}) copy-start(f32[128,128]{1,0:T(8,128)} %param.13) | copy-start | bytes 196612
  977.5 18.9 %copy-start.7 = (f32[128,4]{0,1:T(4,128)S(1)}, f32[128,4]{0,1:T(4,128)}, u32[]{:S(2)}) copy-start(f32[128,4]{0,1:T(4,128)} %param.12) | copy-start | bytes 6148
  978.9 14.9 %collective-permute-start = (bf16[2,2,1,128,4,128]{5,3,4,2,1,0:T(8,128)(2,1)S(1)}, bf16[2,2,1,128,4,128]{5,3,4,2,1,0:T(8,128)(2,1)S(1)}, u32[]{:S(2)}, u32[]{:S(2)}) collective-permute-start(bf16[2,2,1,128,4,128]{5,3,4,2,1,0:T(8,128)(2,1)S(1)} %pad_maximum_fusion.4), channel_id=1, source_target_pairs={{0,16},{16,0},{1,17},{17,1},{2,18},{18,2},{3,19},{19,3},{4,20},{20... | collective-permute-start | bytes 1572872 | tf_op jit(solution)/shard_map/ppermute | solution.py:11
Sparse Core Ops, SparseCore 0:
  8.9 170.7 all-gather.1
where the time goes:
time: 1020 us; the launch traced here: 1010 us
  local copies, waits for them, and re-layouts  259 us (25%)
  blocking collectives  252 us (25%)
  matrix products  246 us (24%)
  waiting for transfers between devices  164 us (16%)
  other arithmetic  61.5 us (6%)
  between operations  13.9 us (1%)
    all_to_all x1, blocking collectives, on_device(): lax.all_to_all(jnp.stack([back_real, back_imag]).astype(jnp.bfloat16), 'm...  200 us
    all_to_all x1, waiting for transfers between devices, on_device(): lax.all_to_all(flattened, 'mom', split_axis=4, concat_axis=3, tiled=True)  151 us
    another operation x6, local copies, waits for them, and re-layouts  58.6 us
    all_to_all x1, blocking collectives, on_device(): lax.all_to_all(weighted, 'pts', split_axis=4, concat_axis=5, tiled=True)  52 us
    another operation x1, local copies, waits for them, and re-layouts, on_device(): jnp.stack([back_real, back_imag]).astype(jnp.bfloat16)  41.2 us
    another operation x3, local copies, waits for them, and re-layouts, complex_mix(): jnp.stack([real_real - left_sign * right_sign * imag_imag, right_sign * r...  40.2 us
    dot_general x4, matrix products, complex_mix(): jnp.einsum(formula, left[1], right[1], preferred_element_type=jnp.float32)  35.8 us
    dot_general x4, matrix products, complex_mix(): jnp.einsum(formula, left[1], right[0], preferred_element_type=jnp.float32)  35.4 us
  transfers between devices with their start and end apart: 3, of which 2 were waited for; matrix products, arithmetic and copies ran while one was open for 53% of the time, Pallas kernels for 0%

commit v1 on v0

--- a/solution.py
+++ b/solution.py
@@ -3,6 +3,15 @@
 import jax.numpy as jnp
 from jax import lax
 from jax.sharding import PartitionSpec as P
+
+
+def task_move(m):
+    reply = lax.psum(1, "mom")
+    part_next = jnp.split(m, reply, axis=3)
+    prior = jnp.stack(part_next)
+    current_value = lax.all_to_all(prior, "mom", 0, 0)
+    u1 = jnp.concatenate(current_value, axis=4)
+    return u1
 
 
 def partner_2(value, axis, apart):
@@ -68,13 +77,7 @@
         jnp.einsum("fs,bnfc->bnsc", cosine_table, prod_imag, preferred_element_type=jnp.float32)
         + jnp.einsum("fs,bnfc->bnsc", sine_table, prod_real, preferred_element_type=jnp.float32)
     ) * inverse_count
-    field_pts = lax.all_to_all(
-        jnp.stack([back_real, back_imag]).astype(jnp.bfloat16),
-        "mom",
-        split_axis=3,
-        concat_axis=4,
-        tiled=True,
-    )
+    field_pts = task_move(jnp.stack([back_real, back_imag]).astype(jnp.bfloat16))
     field_pts = field_pts.reshape(pair_values.shape)
     weighted = complex_mix("bnkum,kvm->bnkvu", field_pts, val_orbitals, 1.0, 1.0).astype(
         jnp.bfloat16

time: 1020 us -> 960 us (0.941)
  local copies, waits for them, and re-layouts: 259 us -> 204 us
  blocking collectives: 252 us -> 238 us
    another operation x7, local copies, waits for them, and re-layouts: 99.8 us -> 66.6 us
    all_to_all x1 -> x0, local copies, waits for them, and re-layouts: 30.2 us -> none  [on_device(): lax.all_to_all(jnp.stack([back_real, back_imag]).astype(jnp.bfloat16), 'm...]
    another operation x1 -> x3, other arithmetic: 1.36 us -> 17.5 us  [the longest x2 16.2 us: task_move(): prior = jnp.stack(part_next)]
    all_to_all x1, blocking collectives: 200 us -> 186 us  [task_move(): current_value = lax.all_to_all(prior, 'mom', 0, 0)]
  transfers between devices with their start and end apart: 3 -> 3, of which waited for: 2 -> 2; matrix products, arithmetic and copies ran while one was open for 53% -> 51% of each run, Pallas kernels for 0% -> 0%
where the time goes in v1:
time: 960 us; the launch traced here: 948 us
  matrix products  246 us (26%)
  blocking collectives  238 us (25%)
  local copies, waits for them, and re-layouts  204 us (21%)
  waiting for transfers between devices  165 us (17%)
  other arithmetic  70.6 us (7%)
  between operations  14.1 us (1%)
  starting transfers between devices  10.2 us (1%)
    all_to_all x1, blocking collectives, task_move(): current_value = lax.all_to_all(prior, 'mom', 0, 0)  186 us
    all_to_all x1, waiting for transfers between devices, on_device(): lax.all_to_all(flattened, 'mom', split_axis=4, concat_axis=3, tiled=True)  151 us
    another operation x6, local copies, waits for them, and re-layouts  59.4 us
    all_to_all x1, blocking collectives, on_device(): lax.all_to_all(weighted, 'pts', split_axis=4, concat_axis=5, tiled=True)  52 us
    another operation x3, local copies, waits for them, and re-layouts, complex_mix(): jnp.stack([real_real - left_sign * right_sign * imag_imag, right_sign * r...  40.2 us
    dot_general x4, matrix products, complex_mix(): jnp.einsum(formula, left[1], right[1], preferred_element_type=jnp.float32)  35.7 us
    dot_general x4, matrix products, complex_mix(): jnp.einsum(formula, left[1], right[0], preferred_element_type=jnp.float32)  35.5 us
    dot_general x4, matrix products, complex_mix(): jnp.einsum(formula, left[0], right[1], preferred_element_type=jnp.float32)  33.9 us
  transfers between devices with their start and end apart: 3, of which 2 were waited for; matrix products, arithmetic and copies ran while one was open for 51% of the time, Pallas kernels for 0%

profile of v1, /device:TPU:0, one launch (start us, length us, event | category | flops | bytes accessed | tf_op | source)
XLA Modules:
  0.0 948.0 jit_solution(10482630740440165149)
XLA Ops:
  30.9 9.8 %fusion.20 = f32[128,2,32,512]{3,2,1,0:T(8,128)} fusion(bf16[2,128,64,32]{2,3,0,1:T(8,128)(2,1)} %fusion.47, bf16[2,128,64,512]{3,2,1,0:T(8,128)(2,1)S(1)} %bitcast.308), kind=kOutput, calls=%fused_computation.40 | convolution fusion | flops 536870912 | bytes 26214400 | tf_op jit(solution)/shard_map/bnkvu,kvm->bnkum/dot_general | solution.py:24
  40.8 14.0 %fusion.37 = bf16[2,1,128,32,512]{4,3,0,2,1:T(8,128)(2,1)} fusion(f32[128,2,32,512]{3,2,1,0:T(8,128)} %fusion.20, bf16[2,128,64,32]{2,3,0,1:T(8,128)(2,1)} %fusion.48, bf16[2,128,64,512]{3,2,1,0:T(8,128)(2,1)} %param.9), kind=kOutput, calls=%fused_computation.57 | convolution fusion | flops 549453824 | bytes 35651584 | tf_op jit(solution)/shard_map/bnkvu,kvm->bnkum/dot_general | solution.py:25
  54.7 16.5 %copy.232 = bf16[2,1,128,32,512]{2,0,4,3,1:T(2,128)(2,1)} copy(bf16[2,1,128,32,512]{4,3,0,2,1:T(8,128)(2,1)} %fusion.37) | data formatting | bytes 16777216 | tf_op jit(solution)/shard_map/stack | solution.py:28
  71.2 12.1 %fusion.26 = f32[128,2,32,512]{3,2,1,0:T(8,128)} fusion(bf16[2,128,64,32]{2,3,0,1:T(8,128)(2,1)S(1)} %copy-done.6, bf16[2,128,64,512]{3,2,1,0:T(8,128)(2,1)} %param.9), kind=kOutput, calls=%fused_computation.46 | convolution fusion | flops 536870912 | bytes 26214400 | tf_op jit(solution)/shard_map/bnkvu,kvm->bnkum/dot_general | solution.py:26
  83.4 12.9 %fusion.40 = bf16[2,1,128,32,512]{4,3,0,2,1:T(8,128)(2,1)} fusion(bf16[2,128,64,32]{2,3,0,1:T(8,128)(2,1)S(1)} %copy-done.4, bf16[2,128,64,512]{3,2,1,0:T(8,128)(2,1)} %param.9, f32[128,2,32,512]{3,2,1,0:T(8,128)} %fusion.26), kind=kOutput, calls=%fused_computation.58 | convolution fusion | flops 549453824 | bytes 34603008 | tf_op jit(solution)/shard_map/bnkvu,kvm->bnkum/dot_general | solution.py:27
  96.3 15.7 %copy.233 = bf16[2,1,128,32,512]{2,0,4,3,1:T(2,128)(2,1)} copy(bf16[2,1,128,32,512]{4,3,0,2,1:T(8,128)(2,1)} %fusion.40) | data formatting | bytes 16777216 | tf_op jit(solution)/shard_map/stack | solution.py:28
  112.0 26.4 %pad_maximum_fusion.1 = bf16[2,2,1,128,16384]{3,1,2,0,4:T(2,128)(2,1)} fusion(bf16[1,2,1,128,16384]{3,1,2,0,4:T(2,128)(2,1)} %bitcast.318, bf16[1,2,1,128,16384]{3,1,2,0,4:T(2,128)(2,1)} %bitcast.317), kind=kLoop, calls=%fused_computation.7 | loop fusion | flops 8388608 | bytes 33554432 | tf_op jit(solution)/shard_map/stack | solution.py:28
  138.4 9.8 %all-to-all-start = ((bf16[2,2,1,128,16384]{3,1,2,0,4:T(2,128)(2,1)}), bf16[2,2,1,128,16384]{3,1,2,0,4:T(2,128)(2,1)}, u32[]{:S(2)}, u32[]{:S(2)}) async-start(bf16[2,2,1,128,16384]{3,1,2,0,4:T(2,128)(2,1)} %pad_maximum_fusion.1), calls=%async_computation | async-start | bytes 33554432 | tf_op jit(solution)/shard_map/all_to_all | solution.py:63
  148.3 12.1 %slice_convert_fusion.1 = (f32[1,256,16,512]{3,2,1,0:T(8,128)}, f32[1,256,16,512]{3,2,1,0:T(8,128)}) fusion(bf16[2,256,16,512]{3,2,1,0:T(8,128)(2,1)} %param.11), kind=kLoop, calls=%fused_computation.67 | loop fusion | flops 4194304 | bytes 25165824 | tf_op jit(solution)/shard_map/convert_element_type | solution.py:70
  160.3 9.9 %copy.231 = f32[1,256,16,512]{1,3,2,0:T(8,128)} copy(f32[1,256,16,512]{3,2,1,0:T(8,128)} %get-tuple-element.17) | data formatting | bytes 16777216 | tf_op jit(solution)/shard_map/convert_element_type | solution.py:70
  170.2 10.0 %copy.234 = f32[1,256,16,512]{1,3,2,0:T(8,128)} copy(f32[1,256,16,512]{3,2,1,0:T(8,128)} %get-tuple-element.18) | data formatting | bytes 16777216 | tf_op jit(solution)/shard_map/convert_element_type | solution.py:70
  180.2 151.0 %all-to-all-done = bf16[2,2,1,128,16384]{3,1,2,0,4:T(2,128)(2,1)} async-done(((bf16[2,2,1,128,16384]{3,1,2,0,4:T(2,128)(2,1)}), bf16[2,2,1,128,16384]{3,1,2,0,4:T(2,128)(2,1)}, u32[]{:S(2)}, u32[]{:S(2)}) %all-to-all-start) | async-done | bytes 16777248 | tf_op jit(solution)/shard_map/all_to_all | solution.py:63
  331.2 28.1 %copy.273 = bf16[2,2,1,128,2,8192]{3,4,5,1,2,0:T(2,128)(2,1)S(1)} copy(bf16[2,2,1,128,2,8192]{3,1,0,5,4,2:T(2,128)(2,1)} %bitcast.38) | data formatting | bytes 33554432 | tf_op jit(solution)/shard_map/all_to_all | solution.py:63
  359.3 13.0 %fusion.136 = (bf16[1,2,1,2,128,8192]{4,3,5,1,2,0:T(2,128)(2,1)}, bf16[1,2,1,2,128,8192]{4,3,5,1,2,0:T(2,128)(2,1)}) fusion(bf16[2,2,1,2,128,8192]{4,3,5,1,2,0:T(2,128)(2,1)S(1)} %bitcast.313), kind=kLoop, calls=%fused_computation.185 | loop fusion | bytes 33554432 | tf_op jit(solution)/shard_map/slice | solution.py:65
  372.3 14.1 %reshape.540 = bf16[2,256,8192]{1,2,0:T(8,128)(2,1)} reshape(bf16[1,2,1,2,128,8192]{4,3,5,1,2,0:T(2,128)(2,1)} %get-tuple-element.16) | data formatting | bytes 16777216 | tf_op jit(solution)/shard_map/reshape.28
  386.4 14.2 %reshape.539 = bf16[2,256,8192]{1,2,0:T(8,128)(2,1)} reshape(bf16[1,2,1,2,128,8192]{4,3,5,1,2,0:T(2,128)(2,1)} %get-tuple-element.15) | data formatting | bytes 16777216 | tf_op jit(solution)/shard_map/reshape.24
  400.6 12.5 %fusion.94 = f32[2,8192,256]{2,1,0:T(8,128)} fusion(bf16[2,256,8192]{1,2,0:T(8,128)(2,1)} %reshape.540, s32[256]{0:T(256)S(1)} %copy-done.8), kind=kOutput, calls=%fused_computation.140 | convolution fusion | flops 2148466688 | bytes 25166848 | tf_op jit(solution)/shard_map/fs,bnsc->bnfc/dot_general | solution.py:67
  422.2 14.8 %convolution_subtract_fusion = f32[2,8192,256]{2,1,0:T(8,128)} fusion(f32[2,8192,256]{2,1,0:T(8,128)} %fusion.94, bf16[2,256,8192]{1,2,0:T(8,128)(2,1)S(1)} %copy-done.1, s32[256]{0:T(256)S(1)} %copy-done.8), kind=kOutput, calls=%fused_computation.26 | convolution fusion | flops 2152660992 | bytes 41944064 | tf_op jit(solution)/shard_map/fs,bnsc->bnfc/dot_general | solution.py:69
  437.0 27.4 %fusion.11 = (bf16[2,256,8192]{1,2,0:T(8,128)(2,1)}, bf16[2,256,8192]{1,2,0:T(8,128)(2,1)}) fusion(f32[2,8192,256]{2,1,0:T(8,128)} %convolution_subtract_fusion, f32[256,8192]{0,1:T(8,128)} %bitcast.312, f32[256,8192]{0,1:T(8,128)} %bitcast.311, f32[2,8192,256]{2,1,0:T(8,128)} %fusion.96, bf16[2,256,8192]{1,2,0:T(8,128)(2,1)} %reshape.540, s32[256]{0:T(256)S(1)} %copy-done.8), kind=kOutput, calls=%fused_computation.30 | convolution fusion | flops 2186215424 | bytes 75498496 | tf_op jit(solution)/shard_map/fs,bnsc->bnfc/dot_general | solution.py:66
  464.4 12.5 %fusion.90 = f32[2,8192,256]{2,1,0:T(8,128)} fusion(bf16[2,256,8192]{1,2,0:T(8,128)(2,1)} %get-tuple-element.11, s32[256]{0:T(256)S(1)} %copy-done.8), kind=kOutput, calls=%fused_computation.138 | convolution fusion | flops 2148466688 | bytes 25166848 | tf_op jit(solution)/shard_map/fs,bnfc->bnsc/dot_general | solution.py:77
  477.0 9.0 fusion.92
  486.0 13.5 %fusion.10 = bf16[1,2,1,256,8192]{3,4,1,2,0:T(8,128)(2,1)} fusion(f32[2,8192,256]{2,1,0:T(8,128)} %fusion.90, bf16[2,256,8192]{1,2,0:T(8,128)(2,1)} %get-tuple-element.12, s32[256]{0:T(256)S(1)} %copy-done.8), kind=kOutput, calls=%fused_computation.29 | convolution fusion | flops 2161049600 | bytes 33555456 | tf_op jit(solution)/shard_map/fs,bnfc->bnsc/dot_general | solution.py:78
  499.5 11.2 %fusion.9 = bf16[1,2,1,256,8192]{3,4,1,2,0:T(8,128)(2,1)} fusion(f32[2,8192,256]{2,1,0:T(8,128)} %fusion.92, bf16[2,256,8192]{1,2,0:T(8,128)(2,1)S(1)} %bitcast.310, s32[256]{0:T(256)S(1)} %copy-done.8), kind=kOutput, calls=%fused_computation.28 | convolution fusion | flops 2161049600 | bytes 33555456 | tf_op jit(solution)/shard_map/fs,bnfc->bnsc/dot_general | solution.py:74
  543.9 185.8 %all_to_all.35 = bf16[2,2,2,1,128,8192]{4,5,2,1,3,0:T(8,128)(2,1)S(1)} all-to-all(bf16[2,2,2,1,128,8192]{4,5,2,1,3,0:T(8,128)(2,1)S(1)} %pad_maximum_fusion.2), channel_id=1, replica_groups=mesh['mom'=2,'pts'=16] {'mom'}, dimensions={0} | all-to-all | bytes 33554432 | tf_op jit(solution)/shard_map/all_to_all | solution.py:12
  743.0 14.7 %copy.201 = bf16[2,128,32,512]{3,2,0,1:T(8,128)(2,1)} copy(bf16[2,128,32,512]{1,3,2,0:T(8,128)(2,1)} %bitcast.315) | data formatting | bytes 16777216 | tf_op jit(solution)/shard_map/reshape.49
  764.9 14.7 %copy.203 = bf16[2,128,32,512]{3,2,0,1:T(8,128)(2,1)} copy(bf16[2,128,32,512]{1,3,2,0:T(8,128)(2,1)} %bitcast.316) | data formatting | bytes 16777216 | tf_op jit(solution)/shard_map/reshape.53
  779.5 10.1 %fusion.17 = f32[128,2,32,64]{3,2,1,0:T(8,128)} fusion(bf16[2,128,32,512]{3,2,0,1:T(8,128)(2,1)} %copy.201, bf16[2,128,64,512]{3,2,1,0:T(8,128)(2,1)} %param.9), kind=kOutput, calls=%fused_computation.37 | convolution fusion | flops 536870912 | bytes 18874368 | tf_op jit(solution)/shard_map/bnkum,kvm->bnkvu/dot_general | solution.py:24
  789.6 10.1 %fusion.15 = f32[128,2,32,64]{3,2,1,0:T(8,128)} fusion(bf16[2,128,32,512]{3,2,0,1:T(8,128)(2,1)} %copy.203, bf16[2,128,64,512]{3,2,1,0:T(8,128)(2,1)} %param.9), kind=kOutput, calls=%fused_computation.35 | convolution fusion | flops 536870912 | bytes 18874368 | tf_op jit(solution)/shard_map/bnkum,kvm->bnkvu/dot_general | solution.py:27
  799.7 9.3 fusion.49
  809.0 10.7 %fusion.50 = bf16[1,2,1,128,64,32]{4,5,1,3,2,0:T(8,128)(2,1)} fusion(f32[128,2,32,64]{3,2,1,0:T(8,128)} %fusion.15, bf16[2,128,32,512]{3,2,0,1:T(8,128)(2,1)} %copy.201, bf16[2,128,64,512]{3,2,1,0:T(8,128)(2,1)} %param.9), kind=kOutput, calls=%fused_computation.75 | convolution fusion | flops 537919488 | bytes 22020096 | tf_op jit(solution)/shard_map/bnkum,kvm->bnkvu/dot_general | solution.py:26
  832.3 52.0 %all_to_all.36 = bf16[2,2,1,128,64,32]{3,5,2,1,0,4:T(8,128)(2,1)S(1)} all-to-all(bf16[2,2,1,128,64,32]{3,5,2,1,0,4:T(8,128)(2,1)S(1)} %copy.206), channel_id=1, replica_groups=mesh['mom'=2,'pts'=16] {'pts'}, dimensions={4} | all-to-all | bytes 4194304 | tf_op jit(solution)/shard_map/all_to_all | solution.py:85
  921.1 12.8 %collective-permute-done = bf16[2,2,1,128,4,128]{5,3,4,2,1,0:T(8,128)(2,1)S(1)} collective-permute-done((bf16[2,2,1,128,4,128]{5,3,4,2,1,0:T(8,128)(2,1)S(1)}, bf16[2,2,1,128,4,128]{5,3,4,2,1,0:T(8,128)(2,1)S(1)}, u32[]{:S(2)}, u32[]{:S(2)}) %collective-permute-start) | collective-permute-done | bytes 524320 | tf_op jit(solution)/shard_map/ppermute | solution.py:20
  (81 shorter events, 142.9 us)
Async XLA Ops:
  6.5 882.9 %all-gather.2.cloned.1.call-start = ((), (), s32[]{:S(2)}) async-start(), calls=%async_computation.3 | async-start | bytes 35651584 | tf_op jit(solution)/shard_map/all_gather | solution.py:89
  7.3 4.6 copy-start.5
  16.0 14.9 %slice-start = ((s8[16777216]{0:T(1024)(128)(4,1)}), s8[4194304]{0:T(1024)(128)(4,1)S(1)}, s32[]{:S(2)}) async-start(s8[16777216]{0:T(1024)(128)(4,1)} %bitcast.307), calls=%async_computation.4 | async-start | bytes 8388608
  16.0 14.9 %slice-start.1 = ((s8[16777216]{0:T(1024)(128)(4,1)}), s8[4194304]{0:T(1024)(128)(4,1)S(1)}, s32[]{:S(2)}) async-start(s8[16777216]{0:T(1024)(128)(4,1)} %bitcast.307), calls=%async_computation.5 | async-start | bytes 8388608
  20.0 10.9 %slice-start.2 = ((s8[16777216]{0:T(1024)(128)(4,1)}), s8[4194304]{0:T(1024)(128)(4,1)S(1)}, s32[]{:S(2)}) async-start(s8[16777216]{0:T(1024)(128)(4,1)} %bitcast.307), calls=%async_computation.6 | async-start | bytes 8388608
  25.5 5.4 slice-start.3
  54.7 16.5 %copy-start.6 = (bf16[2,128,64,32]{2,3,0,1:T(8,128)(2,1)S(1)}, bf16[2,128,64,32]{2,3,0,1:T(8,128)(2,1)}, u32[]{:S(2)}) copy-start(bf16[2,128,64,32]{2,3,0,1:T(8,128)(2,1)} %fusion.47) | copy-start | bytes 3145732
  71.2 12.1 %copy-start.4 = (bf16[2,128,64,32]{2,3,0,1:T(8,128)(2,1)S(1)}, bf16[2,128,64,32]{2,3,0,1:T(8,128)(2,1)}, u32[]{:S(2)}) copy-start(bf16[2,128,64,32]{2,3,0,1:T(8,128)(2,1)} %fusion.48) | copy-start | bytes 3145732
  138.4 192.8 %all-to-all-start = ((bf16[2,2,1,128,16384]{3,1,2,0,4:T(2,128)(2,1)}), bf16[2,2,1,128,16384]{3,1,2,0,4:T(2,128)(2,1)}, u32[]{:S(2)}, u32[]{:S(2)}) async-start(bf16[2,2,1,128,16384]{3,1,2,0,4:T(2,128)(2,1)} %pad_maximum_fusion.1), calls=%async_computation | async-start | bytes 33554432 | tf_op jit(solution)/shard_map/all_to_all | solution.py:63
  386.4 14.2 %copy-start.8 = (s32[256]{0:T(256)S(1)}, s32[256]{0:T(256)}, u32[]{:S(2)}) copy-start(s32[256]{0:T(256)} %param.14) | copy-start | bytes 3076
  400.6 12.6 %copy-start.1 = (bf16[2,256,8192]{1,2,0:T(8,128)(2,1)S(1)}, bf16[2,256,8192]{1,2,0:T(8,128)(2,1)}, u32[]{:S(2)}) copy-start(bf16[2,256,8192]{1,2,0:T(8,128)(2,1)} %reshape.539) | copy-start | bytes 25165828
  464.4 12.6 %copy-start = (bf16[2,256,8192]{1,2,0:T(8,128)(2,1)S(1)}, bf16[2,256,8192]{1,2,0:T(8,128)(2,1)}, u32[]{:S(2)}) copy-start(bf16[2,256,8192]{1,2,0:T(8,128)(2,1)} %get-tuple-element.12) | copy-start | bytes 25165828
  464.4 35.1 %slice-start.4 = ((s8[8388608]{0:T(1024)(128)(4,1)}), s8[4194304]{0:T(1024)(128)(4,1)S(1)}, s32[]{:S(2)}) async-start(s8[8388608]{0:T(1024)(128)(4,1)} %bitcast.309), calls=%async_computation.8 | async-start | bytes 8388608
  477.0 22.6 %slice-start.5 = ((s8[8388608]{0:T(1024)(128)(4,1)}), s8[4194304]{0:T(1024)(128)(4,1)S(1)}, s32[]{:S(2)}) async-start(s8[8388608]{0:T(1024)(128)(4,1)} %bitcast.309), calls=%async_computation.9 | async-start | bytes 8388608
  510.7 8.4 copy-start.2
  510.7 11.3 %copy-start.3 = (bf16[1,2,1,256,8192]{3,4,1,2,0:T(8,128)(2,1)S(1)}, bf16[1,2,1,256,8192]{3,4,1,2,0:T(8,128)(2,1)}, u32[]{:S(2)}) copy-start(bf16[1,2,1,256,8192]{3,4,1,2,0:T(8,128)(2,1)} %fusion.9) | copy-start | bytes 25165828
  910.6 8.9 copy-start.10
  917.6 18.9 %copy-start.7 = (f32[128,128]{1,0:T(8,128)S(1)}, f32[128,128]{1,0:T(8,128)}, u32[]{:S(2)}) copy-start(f32[128,128]{1,0:T(8,128)} %param.13) | copy-start | bytes 196612
  917.7 18.9 %copy-start.9 = (f32[128,4]{0,1:T(4,128)S(1)}, f32[128,4]{0,1:T(4,128)}, u32[]{:S(2)}) copy-start(f32[128,4]{0,1:T(4,128)} %param.12) | copy-start | bytes 6148
  919.1 14.9 %collective-permute-start = (bf16[2,2,1,128,4,128]{5,3,4,2,1,0:T(8,128)(2,1)S(1)}, bf16[2,2,1,128,4,128]{5,3,4,2,1,0:T(8,128)(2,1)S(1)}, u32[]{:S(2)}, u32[]{:S(2)}) collective-permute-start(bf16[2,2,1,128,4,128]{5,3,4,2,1,0:T(8,128)(2,1)S(1)} %pad_maximum_fusion.5), channel_id=1, source_target_pairs={{0,16},{16,0},{1,17},{17,1},{2,18},{18,2},{3,19},{19,3},{4,20},{20... | collective-permute-start | bytes 1572872 | tf_op jit(solution)/shard_map/ppermute | solution.py:20
Sparse Core Ops, SparseCore 0:
  8.9 170.7 all-gather.1
